TPU v7x, 32 devices: a whole 2x2x4 slice. The times are simulated.
32 devices in a mesh: dp: 8 (over z, y), tensor: 4 (over x, core).
Axes of the slice: x: 2, y: 2, z: 4, core: 2. Of those that a mesh axis runs over, the one named last changes fastest.
Arguments:
- inputs: bfloat16 [4096, 768], P(('dp', 'tensor')), may hold values from -6 to 6
- prev_logits: bfloat16 [4096, 12, 4096], P('dp', 'tensor'), may hold values from -6 to 6
- w_query: bfloat16 [768, 768], P('dp', 'tensor'), may hold values from -0.21875 to 0.21875
- w_key: bfloat16 [768, 768], P('dp', 'tensor'), may hold values from -0.21875 to 0.21875
- w_value: bfloat16 [768, 768], P('dp', 'tensor'), may hold values from -0.21875 to 0.21875
- w_attn_out: bfloat16 [768, 768], P('tensor', 'dp'), may hold values from -2.5 to 2.5
- w_ffn_in: bfloat16 [768, 3072], P('dp', 'tensor'), may hold values from -0.21875 to 0.21875
- ffn_bias: bfloat16 [3072], P(('tensor', 'dp')), may hold values from -3 to 3
- w_ffn_out: bfloat16 [3072, 768], P(('tensor', 'dp')), may hold values from -0.109375 to 0.109375
- norm1_gain: float32 [768], replicated, may hold values from 0.5 to 1.5
- norm1_shift: float32 [768], replicated, may hold values from -2 to 2
- norm2_gain: float32 [768], replicated, may hold values from 0.5 to 1.5
- norm2_shift: float32 [768], replicated, may hold values from -2 to 2
- token_segment: int32 [4096], replicated, may hold values from 0 to 12, as said below
- segment_parent: int32 [1, 13], replicated, may hold values from 0 to 4, as said below
- out_grad: bfloat16 [4096, 768], P(('dp', 'tensor')), may hold values from -6 to 6
- logit_grad: bfloat16 [4096, 12, 4096], P('dp', 'tensor'), may hold values from -6 to 6
Outputs:
- output: bfloat16 [4096, 768], P(('dp', 'tensor'))
- logits: bfloat16 [4096, 12, 4096], P('dp', 'tensor')
- input_grad: float32 [4096, 768], P(('dp', 'tensor'))
- prev_grad: bfloat16 [4096, 12, 4096], P('dp', 'tensor')
- w_query_grad: float32 [768, 768], P('dp', 'tensor')
- w_key_grad: float32 [768, 768], P('dp', 'tensor')
- w_value_grad: float32 [768, 768], P('dp', 'tensor')
- w_attn_out_grad: float32 [768, 768], P('tensor', 'dp')
- w_ffn_in_grad: float32 [768, 3072], P('dp', 'tensor')
- ffn_bias_grad: float32 [3072], P(('tensor', 'dp'))
- w_ffn_out_grad: float32 [3072, 768], P(('tensor', 'dp'))
- norm1_gain_grad: float32 [768], replicated
- norm1_shift_grad: float32 [768], replicated
- norm2_gain_grad: float32 [768], replicated
- norm2_shift_grad: float32 [768], replicated
Inputs may be any that keep to these rules, and one draw needn't show every extreme that they name: `token_segment`: in each tree the first 2048 tokens are segment 0, the trunk; the other tokens hold the 4 branches (segments 1 to 4, 256 tokens each) and the 8 leaves (segments 5 to 12, 128 tokens each), each segment one contiguous run, in an order that varies from tree to tree. `segment_parent`: row t lists the parents of tree t's segments: 0 for the trunk and every branch, a branch for every leaf, each branch the parent of exactly two leaves.
All inputs are finite; a program needn't handle non-finite values.
Results may differ from a plain program's by a relative error of at most 0.017.
Values may be sent and summed in bfloat16 or wider, within the bound.
No kernel may reach another device: no remote copies, remote signals or barrier semaphores. Data moves between devices by JAX's collectives and lax.ppermute only.
A program may use at most 256 MiB of HBM per device.

v0:
```python
import jax
import jax.numpy as jnp
from jax import lax
from jax.sharding import PartitionSpec as P

E = 64
EPSILON = 1e-12


def layer_norm(values, norm_gain, norm_shift):
    center = values - jnp.mean(values, axis=-1, keepdims=True)
    spread = jnp.mean(center * center, axis=-1, keepdims=True)
    return center * lax.rsqrt(spread + EPSILON) * norm_gain + norm_shift


def gelu_exact(values):
    return jax.nn.gelu(values, approximate=False)


def attend_forward(key_count, local_heads, head_dim, score_scale):
    columns = local_heads * head_dim

    def run(operands):
        query_heads, tree_kv, previous, allowed = operands
        group_rows = query_heads.shape[0]
        key_heads = tree_kv[:key_count, :columns].reshape(key_count, local_heads, head_dim)
        value_heads = tree_kv[:key_count, columns:].reshape(key_count, local_heads, head_dim)
        scores = jnp.einsum(
            "qhe,khe->qhk", query_heads, key_heads, preferred_element_type=jnp.float32
        ) * score_scale + previous.astype(jnp.float32)
        logits = jnp.where(allowed, scores, 0.0).astype(jnp.bfloat16)
        masked = jnp.where(allowed, scores, -jnp.inf)
        row_max = jnp.max(masked, axis=-1, keepdims=True)
        exponent = jnp.exp(masked - row_max)
        row_total = jnp.sum(exponent, axis=-1, keepdims=True)
        log_total = row_max + jnp.log(row_total)
        weights = (exponent / row_total).astype(jnp.bfloat16)
        mixed = (
            jnp.einsum("qhk,khe->qhe", weights, value_heads, preferred_element_type=jnp.float32)
            .astype(jnp.bfloat16)
            .reshape(group_rows, columns)
        )
        return (mixed, logits, log_total)

    return run


def attend_backward(key_count, local_heads, head_dim, score_scale):
    columns = local_heads * head_dim

    def run(operands):
        query_heads, tree_kv, previous, allowed, log_total, grad_mixed_heads, upstream = operands
        group_rows = query_heads.shape[0]
        key_heads = tree_kv[:key_count, :columns].reshape(key_count, local_heads, head_dim)
        value_heads = tree_kv[:key_count, columns:].reshape(key_count, local_heads, head_dim)
        scores = jnp.einsum(
            "qhe,khe->qhk", query_heads, key_heads, preferred_element_type=jnp.float32
        ) * score_scale + previous.astype(jnp.float32)
        attention_weight = jnp.exp(jnp.where(allowed, scores, -jnp.inf) - log_total)
        grad_weight = jnp.einsum(
            "qhe,khe->qhk", grad_mixed_heads, value_heads, preferred_element_type=jnp.float32
        )
        grad_values = jnp.einsum(
            "qhk,qhe->khe",
            attention_weight.astype(jnp.bfloat16),
            grad_mixed_heads,
            preferred_element_type=jnp.float32,
        )
        grad_soft = attention_weight * (
            grad_weight - jnp.sum(attention_weight * grad_weight, axis=-1, keepdims=True)
        )
        grad_scores = jnp.where(allowed, upstream.astype(jnp.float32) + grad_soft, 0.0).astype(
            jnp.bfloat16
        )
        grad_query = (
            (
                jnp.einsum(
                    "qhk,khe->qhe", grad_scores, key_heads, preferred_element_type=jnp.float32
                )
                * score_scale
            )
            .astype(jnp.bfloat16)
            .reshape(group_rows, columns)
        )
        grad_keys = (
            jnp.einsum("qhk,qhe->khe", grad_scores, query_heads, preferred_element_type=jnp.float32)
            * score_scale
        )
        tree_grads = jnp.concatenate(
            [grad_keys.reshape(key_count, columns), grad_values.reshape(key_count, columns)], axis=1
        )
        return (grad_scores, grad_query, tree_grads)

    return run


def shards(
    inputs,
    prev_logits,
    w_query,
    w_key,
    w_value,
    w_attn_out,
    w_ffn_in,
    ffn_bias,
    w_ffn_out,
    norm1_gain,
    norm1_shift,
    norm2_gain,
    norm2_shift,
    token_segment,
    segment_parent,
    out_grad,
    logit_grad,
):
    group_rows = prev_logits.shape[0]
    local_heads = prev_logits.shape[1]
    tree_len = prev_logits.shape[2]
    head_dim = E
    columns = local_heads * head_dim
    spread = tree_len // group_rows
    score_scale = head_dim ** (-0.5)
    data_index = lax.axis_index("dp")
    tree_index = data_index // spread
    local_index = data_index % spread
    query_start = local_index * group_rows
    full_query, full_key, full_value, full_attn, full_inner, full_bias, full_outer = (
        lax.all_gather(w_query, "dp", axis=0, tiled=True),
        lax.all_gather(w_key, "dp", axis=0, tiled=True),
        lax.all_gather(w_value, "dp", axis=0, tiled=True),
        lax.all_gather(w_attn_out, "dp", axis=1, tiled=True),
        lax.all_gather(w_ffn_in, "dp", axis=0, tiled=True),
        lax.all_gather(ffn_bias, "dp", axis=0, tiled=True),
        lax.all_gather(w_ffn_out, "dp", axis=0, tiled=True),
    )
    full_project = jnp.concatenate([full_query, full_key, full_value], axis=1)
    rows_all = lax.all_gather(inputs, "tensor", axis=0, tiled=True)
    projected = jnp.dot(rows_all, full_project, preferred_element_type=jnp.float32).astype(
        jnp.bfloat16
    )
    query = projected[:, :columns]
    kv_local = projected[:, columns:]
    everything = lax.all_gather(kv_local, "dp", axis=0, tiled=True)
    tree_kv = lax.dynamic_slice_in_dim(everything, tree_index * tree_len, tree_len, 0)
    seg_tree = lax.dynamic_slice_in_dim(token_segment, tree_index * tree_len, tree_len, 0)
    seg_rows = lax.dynamic_slice_in_dim(seg_tree, query_start, group_rows, 0)
    parents = lax.dynamic_slice_in_dim(segment_parent, tree_index, 1, 0)[0]
    labels = jnp.arange(parents.shape[0], dtype=jnp.int32)
    parent_one = jnp.sum(
        jnp.where(seg_rows[:, None] == labels[None, :], parents[None, :], 0), axis=1
    )
    parent_two = jnp.sum(
        jnp.where(parent_one[:, None] == labels[None, :], parents[None, :], 0), axis=1
    )
    allowed = (
        (seg_tree[None, :] == seg_rows[:, None])
        | (seg_tree[None, :] == parent_one[:, None])
        | (seg_tree[None, :] == parent_two[:, None])
    )[:, None, :]
    query_heads = query.reshape(group_rows, local_heads, head_dim)
    forward_all = attend_forward(tree_len, local_heads, head_dim, score_scale)
    forward_operands = (query_heads, tree_kv, prev_logits, allowed)
    mixed, logits, log_total = forward_all(forward_operands)
    attended = lax.psum_scatter(
        jnp.dot(mixed, full_attn, preferred_element_type=jnp.float32).astype(jnp.bfloat16),
        "tensor",
        scatter_dimension=0,
        tiled=True,
    ).astype(jnp.float32)
    first_sum = inputs.astype(jnp.float32) + attended
    hidden, norm_one_back = jax.vjp(layer_norm, first_sum, norm1_gain, norm1_shift)
    hidden_all = lax.all_gather(hidden.astype(jnp.bfloat16), "tensor", axis=0, tiled=True)
    inner_raw = jnp.dot(
        hidden_all, full_inner, preferred_element_type=jnp.float32
    ) + full_bias.astype(jnp.float32)
    active, gelu_back = jax.vjp(gelu_exact, inner_raw)
    active_low = active.astype(jnp.bfloat16)
    ffn_out = lax.psum_scatter(
        jnp.dot(active_low, full_outer, preferred_element_type=jnp.float32).astype(jnp.bfloat16),
        "tensor",
        scatter_dimension=0,
        tiled=True,
    ).astype(jnp.float32)
    result, norm_two_back = jax.vjp(layer_norm, hidden + ffn_out, norm2_gain, norm2_shift)
    grad_second, grad_gain_two, grad_shift_two = norm_two_back(out_grad.astype(jnp.float32))
    grad_rows_all = lax.all_gather(grad_second.astype(jnp.bfloat16), "tensor", axis=0, tiled=True)
    grad_active = jnp.dot(grad_rows_all, full_outer.T, preferred_element_type=jnp.float32).astype(
        jnp.bfloat16
    )
    grad_w_outer = jnp.dot(active_low.T, grad_rows_all, preferred_element_type=jnp.float32)
    (grad_inner,) = gelu_back(grad_active.astype(jnp.float32))
    grad_inner_low = grad_inner.astype(jnp.bfloat16)
    grad_bias = jnp.sum(grad_inner_low.astype(jnp.float32), axis=0)
    grad_w_inner = jnp.dot(hidden_all.T, grad_inner_low, preferred_element_type=jnp.float32)
    grad_hidden = grad_second + lax.psum_scatter(
        jnp.dot(grad_inner_low, full_inner.T, preferred_element_type=jnp.float32).astype(
            jnp.bfloat16
        ),
        "tensor",
        scatter_dimension=0,
        tiled=True,
    ).astype(jnp.float32)
    grad_first, grad_gain_one, grad_shift_one = norm_one_back(grad_hidden)
    grad_attn_all = lax.all_gather(grad_first.astype(jnp.bfloat16), "tensor", axis=0, tiled=True)
    grad_mixed = jnp.dot(grad_attn_all, full_attn.T, preferred_element_type=jnp.float32).astype(
        jnp.bfloat16
    )
    grad_w_attn = jnp.dot(mixed.T, grad_attn_all, preferred_element_type=jnp.float32)
    grad_mixed_heads = grad_mixed.reshape(group_rows, local_heads, head_dim)
    backward_all = attend_backward(tree_len, local_heads, head_dim, score_scale)
    backward_operands = (
        query_heads,
        tree_kv,
        prev_logits,
        allowed,
        log_total,
        grad_mixed_heads,
        logit_grad,
    )
    grad_scores, grad_query, tree_grads = backward_all(backward_operands)
    placed = lax.dynamic_update_slice_in_dim(
        jnp.zeros((lax.axis_size("dp") * group_rows, 2 * columns), jnp.float32),
        tree_grads,
        tree_index * tree_len,
        0,
    )
    own_grads = lax.psum_scatter(placed, "dp", scatter_dimension=0, tiled=True)
    grad_project = jnp.concatenate([grad_query, own_grads.astype(jnp.bfloat16)], axis=1)
    grad_w_project = jnp.dot(rows_all.T, grad_project, preferred_element_type=jnp.float32)
    grad_inputs = grad_first + lax.psum_scatter(
        jnp.dot(grad_project, full_project.T, preferred_element_type=jnp.float32).astype(
            jnp.bfloat16
        ),
        "tensor",
        scatter_dimension=0,
        tiled=True,
    ).astype(jnp.float32)
    weight_grads = (
        lax.psum_scatter(grad_w_project[:, :columns], "dp", scatter_dimension=0, tiled=True),
        lax.psum_scatter(
            grad_w_project[:, columns : 2 * columns], "dp", scatter_dimension=0, tiled=True
        ),
        lax.psum_scatter(grad_w_project[:, 2 * columns :], "dp", scatter_dimension=0, tiled=True),
        lax.psum_scatter(grad_w_attn, "dp", scatter_dimension=1, tiled=True),
        lax.psum_scatter(grad_w_inner, "dp", scatter_dimension=0, tiled=True),
        lax.psum_scatter(grad_bias, "dp", scatter_dimension=0, tiled=True),
        lax.psum_scatter(grad_w_outer, "dp", scatter_dimension=0, tiled=True),
    )
    norm_grads = lax.psum(
        (grad_gain_one, grad_shift_one, grad_gain_two, grad_shift_two), ("dp", "tensor")
    )
    return (
        result.astype(jnp.bfloat16),
        logits,
        grad_inputs,
        grad_scores,
        weight_grads[0],
        weight_grads[1],
        weight_grads[2],
        weight_grads[3],
        weight_grads[4],
        weight_grads[5],
        weight_grads[6],
        norm_grads[0],
        norm_grads[1],
        norm_grads[2],
        norm_grads[3],
    )


def solution(mesh):
    placed = (
        P(("dp", "tensor"), None),
        P("dp", "tensor", None),
        P("dp", "tensor"),
        P("dp", "tensor"),
        P("dp", "tensor"),
        P("tensor", "dp"),
        P("dp", "tensor"),
        P(("tensor", "dp")),
        P(("tensor", "dp"), None),
        P(),
        P(),
        P(),
        P(),
        P(),
        P(),
        P(("dp", "tensor"), None),
        P("dp", "tensor", None),
    )
    return jax.shard_map(
        shards,
        mesh=mesh,
        in_specs=placed,
        out_specs=(
            P(("dp", "tensor"), None),
            P("dp", "tensor", None),
            P(("dp", "tensor"), None),
            P("dp", "tensor", None),
            P("dp", "tensor"),
            P("dp", "tensor"),
            P("dp", "tensor"),
            P("tensor", "dp"),
            P("dp", "tensor"),
            P(("tensor", "dp")),
            P(("tensor", "dp"), None),
            P(),
            P(),
            P(),
            P(),
        ),
        check_vma=False,
    )
```

profile of v0, /device:TPU:0, one launch (start us, length us, event | category | flops | bytes accessed | tf_op | source)
XLA Modules:
  0.0 1029.3 jit_solution(4397699468486531703)
XLA Ops:
  7.2 33.0 %all_gather.36 = bf16[768,192]{1,0:T(8,128)(2,1)S(1)} all-gather(bf16[96,192]{1,0:T(8,128)(2,1)} %param.19), channel_id=1, replica_groups=mesh['dp'=8,'tensor'=4] {'dp'}, dimensions={0}, use_global_device_ids=true | all-gather | bytes 331776 | tf_op jit(solution)/shard_map/all_gather | solution.py:128
  40.2 31.4 %all_gather.37 = bf16[768,192]{1,0:T(8,128)(2,1)S(1)} all-gather(bf16[96,192]{1,0:T(8,128)(2,1)} %param.20), channel_id=1, replica_groups=mesh['dp'=8,'tensor'=4] {'dp'}, dimensions={0}, use_global_device_ids=true | all-gather | bytes 331776 | tf_op jit(solution)/shard_map/all_gather | solution.py:129
  71.6 31.2 %all_gather.38 = bf16[768,192]{1,0:T(8,128)(2,1)S(1)} all-gather(bf16[96,192]{1,0:T(8,128)(2,1)} %param.21), channel_id=1, replica_groups=mesh['dp'=8,'tensor'=4] {'dp'}, dimensions={0}, use_global_device_ids=true | all-gather | bytes 331776 | tf_op jit(solution)/shard_map/all_gather | solution.py:130
  102.7 8.8 all_gather.39
  113.6 16.6 %copy.55 = bf16[512,3,4096]{0,2,1:T(8,128)(2,1)} copy(bf16[512,3,4096]{2,0,1:T(8,128)(2,1)} %param.18) | data formatting | bytes 25165824 | tf_op args[1]
  130.5 32.3 %all_gather.41 = bf16[192,768]{0,1:T(8,128)(2,1)S(1)} all-gather(bf16[192,96]{0,1:T(8,128)(2,1)S(1)} %copy.57), channel_id=1, replica_groups=mesh['dp'=8,'tensor'=4] {'dp'}, dimensions={1}, use_global_device_ids=true | all-gather | bytes 331776 | tf_op jit(solution)/shard_map/all_gather | solution.py:131
  162.8 3.5 compare_or_fusion
  166.3 14.6 %all-gather.4.cloned.1.call-done = bf16[4096,384]{0,1:T(8,128)(2,1)} async-done(((bf16[512,384]{0,1:T(8,128)(2,1)}), bf16[4096,384]{0,1:T(8,128)(2,1)}) %all-gather.4.cloned.1.call-update) | async-done | bytes 3145744 | tf_op jit(solution)/shard_map/all_gather | solution.py:143
  180.9 2.3 fusion.52
  183.4 14.6 %select_reduce_fusion = (f32[512,3]{0,1:T(4,128)S(1)}, f32[512,3,4096]{0,2,1:T(8,128)}) fusion(pred[512,4096]{0,1:T(8,128)(4,1)S(1)} %copy-done, bf16[512,3,4096]{0,2,1:T(8,128)(2,1)} %copy.55, bf16[4096,3,64]{0,2,1:T(8,128)(2,1)S(1)} %bitcast.77, bf16[512,3,64]{0,2,1:T(8,128)(2,1)S(1)} %bitcast.85), kind=kOutput, calls=%fused_computation.13 | convolution fusion | flops 836762112 | bytes 41621504 | tf_op jit(solution)/shard_map/qhe,khe->qhk/dot_general | solution.py:28
  198.0 11.0 %fusion.5 = f32[512,3]{0,1:T(4,128)S(1)} fusion(f32[512,3,4096]{0,2,1:T(8,128)} %get-tuple-element.87, f32[512,3]{0,1:T(4,128)S(1)} %get-tuple-element.86, pred[512,4096]{0,1:T(8,128)(4,1)S(1)} %copy-done), kind=kLoop, calls=%fused_computation.12 | loop fusion | flops 18872832 | bytes 27275264 | tf_op jit(solution)/shard_map/reduce_sum | solution.py:35
  209.0 11.5 %fusion.29 = bf16[3,64,512]{2,1,0:T(8,128)(2,1)S(1)} fusion(bf16[4096,3,64]{0,2,1:T(8,128)(2,1)S(1)} %bitcast.83, f32[512,3,4096]{0,2,1:T(8,128)} %get-tuple-element.87, f32[512,3]{0,1:T(4,128)S(1)} %fusion.5, f32[512,3]{0,1:T(4,128)S(1)} %get-tuple-element.86, pred[512,4096]{0,1:T(8,128)(4,1)S(1)} %copy-done), kind=kOutput, calls=%fused_computation.63 | convolution fusion | flops 830570496 | bytes 29044736 | tf_op jit(solution)/shard_map/qhk,khe->qhe/dot_general | solution.py:39
  225.4 17.8 %all-reduce = bf16[768]{0:T(1024)(128)(2,1)S(1)} all-reduce(bf16[768]{0:T(1024)(128)(2,1)S(1)} %dynamic-update-slice), channel_id=1, replica_groups=mesh['dp'=8,'tensor'=4] {'dp'}, use_global_device_ids=true, to_apply=%add | all-reduce | flops 768 | bytes 3072
  247.1 8.7 all_gather.42
  255.8 31.5 %all-gather.6.cloned.1.call-done = bf16[768,768]{1,0:T(8,128)(2,1)} async-done(((bf16[96,768]{1,0:T(8,128)(2,1)}), bf16[768,768]{1,0:T(8,128)(2,1)}) %all-gather.6.cloned.1.call-update) | async-done | bytes 1179664 | tf_op jit(solution)/shard_map/all_gather | solution.py:132
  287.3 6.5 multiply_convert_fusion
  293.8 35.6 %all-gather.8.cloned.1.call-done = bf16[768,768]{1,0:T(8,128)(2,1)} async-done(((bf16[96,768]{1,0:T(8,128)(2,1)}), bf16[768,768]{1,0:T(8,128)(2,1)}) %all-gather.8.cloned.1.call-update) | async-done | bytes 1179664 | tf_op jit(solution)/shard_map/all_gather | solution.py:134
  329.4 3.3 convolution_convert_fusion.2
  332.8 22.1 %reduce-scatter.22.cloned.1.call-done = bf16[128,768]{1,0:T(8,128)(2,1)} async-done(((bf16[512,768]{1,0:T(8,128)(2,1)}), bf16[128,768]{1,0:T(8,128)(2,1)}) %reduce-scatter.22.cloned.1.call-update) | async-done | bytes 196624 | tf_op jit(solution)/shard_map/reduce_scatter | solution.py:178
  357.7 8.2 all_gather.46
  365.9 1.8 convert_reduce_fusion
  368.6 1.7 convolution_convert_fusion
  370.4 16.6 %copy.58 = bf16[512,3,4096]{0,2,1:T(8,128)(2,1)} copy(bf16[512,3,4096]{2,0,1:T(8,128)(2,1)} %param.33) | data formatting | bytes 25165824 | tf_op args[16]
  387.6 6.5 reduce-scatter.24.cloned.1.call-done
  394.1 1.8 multiply_reduce_fusion
  397.4 8.5 all_gather.47
  407.0 13.0 %fusion.7 = f32[3,64,4096]{2,1,0:T(8,128)} fusion(bf16[512,3,64]{0,2,1:T(8,128)(2,1)S(1)} %bitcast.89, f32[512,3,4096]{0,2,1:T(8,128)} %get-tuple-element.87, f32[512,3]{0,1:T(4,128)S(1)} %copy-done.31, pred[512,4096]{0,1:T(8,128)(4,1)S(1)} %copy-done.1), kind=kOutput, calls=%fused_computation.15 | convolution fusion | flops 824180736 | bytes 30611456 | tf_op jit(solution)/shard_map/qhk,qhe->khe/dot_general | solution.py:63
  420.0 38.9 %fusion.4 = bf16[512,3,4096]{0,2,1:T(8,128)(2,1)} fusion(bf16[512,3,4096]{0,2,1:T(8,128)(2,1)} %copy.58, f32[512,3,4096]{0,2,1:T(8,128)} %get-tuple-element.87, f32[512,3]{0,1:T(4,128)} %log_add_fusion, pred[512,4096]{0,1:T(8,128)(4,1)} %compare_or_fusion, bf16[4096,3,64]{0,2,1:T(8,128)(2,1)} %bitcast.84, bf16[512,3,64]{0,2,1:T(8,128)(2,1)} %bitcast.90), kind=kOutput, calls=%fused_computation.6 | convolution fusion | flops 1679824384 | bytes 54204416 | tf_op jit(solution)/shard_map/sub | solution.py:70
  458.9 8.7 convolution_multiply_fusion
  467.6 3.1 pad_maximum_fusion
  470.8 2.3 convolution_bitcast_fusion.1
  473.3 6.8 fusion.28
  480.2 109.5 %reduce-scatter.26.cloned.1.call-done = f32[512,384]{0,1:T(8,128)} async-done(((f32[4096,384]{0,1:T(8,128)}), f32[512,384]{0,1:T(8,128)}) %reduce-scatter.26.cloned.1.call-update) | async-done | bytes 786448 | tf_op jit(solution)/shard_map/reduce_scatter | solution.py:227
  590.9 3.3 convolution_convert_fusion.3
  594.2 2.2 fusion.56
  597.6 2.3 fusion.55
  606.1 14.9 %select_convert_fusion = bf16[512,3,4096]{0,2,1:T(8,128)(2,1)} fusion(f32[512,3,4096]{0,2,1:T(8,128)} %get-tuple-element.87, pred[512,4096]{0,1:T(8,128)(4,1)S(1)} %copy-done.2), kind=kLoop, calls=%fused_computation.9 | loop fusion | flops 6291456 | bytes 39845888 | tf_op jit(solution)/shard_map/convert_element_type | solution.py:31
  621.1 16.9 %copy.62 = bf16[512,3,4096]{2,0,1:T(8,128)(2,1)} copy(bf16[512,3,4096]{0,2,1:T(8,128)(2,1)} %select_convert_fusion) | data formatting | bytes 25165824
  638.0 19.7 %all-reduce.1 = f32[768]{0:T(1024)S(1)} all-reduce(f32[768]{0:T(1024)S(1)} %copy-done.34), channel_id=12, replica_groups=mesh['dp'=8,'tensor'=4] {'dp'}, use_global_device_ids=true, to_apply=%region_24.25.clone | all-reduce | flops 768 | bytes 6144
  658.3 16.9 %copy.63 = bf16[512,3,4096]{2,0,1:T(8,128)(2,1)} copy(bf16[512,3,4096]{0,2,1:T(8,128)(2,1)} %fusion.4) | data formatting | bytes 25165824
  675.2 38.2 %all-reduce.2 = (f32[768]{0:T(1024)}, f32[768]{0:T(1024)}, f32[768]{0:T(1024)}, f32[768]{0:T(1024)}) all-reduce(f32[768]{0:T(1024)S(1)} %get-tuple-element.60, f32[768]{0:T(1024)S(1)} %copy-done.28, f32[768]{0:T(1024)S(1)} %get-tuple-element.62, f32[768]{0:T(1024)S(1)} %get-tuple-element.65), channel_id=1, replica_groups=mesh['dp'=8,'tensor'=4] {'dp','tensor'}, use_global_device_ids=true, to_apply=%region_27.28 | all-reduce | flops 3072 | bytes 24576 | tf_op jit(solution)/shard_map/psum | solution.py:249
  713.5 1.6 copy.78
  715.1 1.8 convert_add_fusion
  716.9 36.8 %reduce-scatter.32.cloned.1.call-done = f32[96,768]{1,0:T(8,128)} async-done(((f32[768,768]{1,0:T(8,128)}), f32[96,768]{1,0:T(8,128)}) %reduce-scatter.32.cloned.1.call-update) | async-done | bytes 294928 | tf_op jit(solution)/shard_map/reduce_scatter | solution.py:247
  753.7 72.6 %reduce-scatter.30.cloned.1.call-done = f32[96,768]{1,0:T(8,128)} async-done(((f32[768,768]{1,0:T(8,128)}), f32[96,768]{1,0:T(8,128)}) %reduce-scatter.30.cloned.1.call-update) | async-done | bytes 294928 | tf_op jit(solution)/shard_map/reduce_scatter | solution.py:245
  826.3 65.6 %reduce-scatter.38.cloned.1.call-done = f32[96,192]{1,0:T(8,128)} async-done(((f32[768,192]{1,0:T(8,128)}), f32[96,192]{1,0:T(8,128)}) %reduce-scatter.38.cloned.1.call-update) | async-done | bytes 73744
  891.9 65.3 %reduce-scatter.36.cloned.1.call-done = f32[96,192]{1,0:T(8,128)} async-done(((f32[768,192]{1,0:T(8,128)}), f32[96,192]{1,0:T(8,128)}) %reduce-scatter.36.cloned.1.call-update) | async-done | bytes 73744
  957.1 65.4 %reduce-scatter.34.cloned.1.call-done = f32[96,192]{1,0:T(8,128)} async-done(((f32[768,192]{1,0:T(8,128)}), f32[96,192]{1,0:T(8,128)}) %reduce-scatter.34.cloned.1.call-update) | async-done | bytes 73744
  (158 shorter events, 26.1 us)
Async XLA Ops:
  7.2 173.7 %all-gather.4.cloned.1.call-start = ((), (), s32[]{:S(2)}) async-start(), calls=%async_computation.11 | async-start | bytes 3538944 | tf_op jit(solution)/shard_map/all_gather | solution.py:143
  40.2 72.4 %copy-start.19 = (bf16[768,192]{1,0:T(8,128)(2,1)}, bf16[768,192]{1,0:T(8,128)(2,1)S(1)}, u32[]{:S(2)}) copy-start(bf16[768,192]{1,0:T(8,128)(2,1)S(1)} %all_gather.36) | copy-start | bytes 884740
  71.6 41.0 %copy-start.20 = (bf16[768,192]{1,0:T(8,128)(2,1)}, bf16[768,192]{1,0:T(8,128)(2,1)S(1)}, u32[]{:S(2)}) copy-start(bf16[768,192]{1,0:T(8,128)(2,1)S(1)} %all_gather.37) | copy-start | bytes 884740
  102.7 9.8 copy-start.21
  113.4 130.4 %reduce-scatter.20.cloned.1.call-start = ((), (), s32[]{:S(2)}) async-start(), calls=%async_computation.12 | async-start | bytes 983040 | tf_op jit(solution)/shard_map/reduce_scatter | solution.py:164
  113.5 69.7 %copy-start.14 = (bf16[512,192]{0,1:T(8,128)(2,1)}, bf16[512,192]{0,1:T(8,128)(2,1)S(1)}, u32[]{:S(2)}) copy-start(bf16[512,192]{0,1:T(8,128)(2,1)S(1)} %slice.33) | copy-start | bytes 589828
  113.6 16.7 %copy-start.25 = (s32[4096]{0:T(1024)S(1)}, s32[4096]{0:T(1024)}, u32[]{:S(2)}) copy-start(s32[4096]{0:T(1024)} %param.30) | copy-start | bytes 49156
  113.6 16.7 %copy-start.37 = (s32[1,13]{1,0:T(1,128)S(1)}, s32[1,13]{1,0:T(1,128)}, u32[]{:S(2)}) copy-start(s32[1,13]{1,0:T(1,128)} %param.31) | copy-start | bytes 160
  162.8 57.8 %copy-start.5 = (bf16[192,768]{0,1:T(8,128)(2,1)}, bf16[192,768]{0,1:T(8,128)(2,1)S(1)}, u32[]{:S(2)}) copy-start(bf16[192,768]{0,1:T(8,128)(2,1)S(1)} %all_gather.41) | copy-start | bytes 884740
  183.2 25.8 %copy-start.13 = (bf16[4096,192]{0,1:T(8,128)(2,1)}, bf16[4096,192]{0,1:T(8,128)(2,1)S(1)}, u32[]{:S(2)}) copy-start(bf16[4096,192]{0,1:T(8,128)(2,1)S(1)} %get-tuple-element.79) | copy-start | bytes 4718596
  220.5 3.4 copy-start.38
  220.5 4.6 copy-start.41
  220.5 23.3 %copy-start.3 = (bf16[128,768]{1,0:T(8,128)(2,1)S(1)}, bf16[128,768]{1,0:T(8,128)(2,1)}, u32[]{:S(2)}) copy-start(bf16[128,768]{1,0:T(8,128)(2,1)} %param.17) | copy-start | bytes 589828
  221.2 24.8 %copy-start.23 = (f32[768]{0:T(1024)S(1)}, f32[768]{0:T(1024)}, u32[]{:S(2)}) copy-start(f32[768]{0:T(1024)} %param.26) | copy-start | bytes 9220
  221.2 24.8 %copy-start.26 = (f32[768]{0:T(1024)S(1)}, f32[768]{0:T(1024)}, u32[]{:S(2)}) copy-start(f32[768]{0:T(1024)} %param.27) | copy-start | bytes 9220
  222.5 64.8 %all-gather.6.cloned.1.call-start = ((), (), s32[]{:S(2)}) async-start(), calls=%async_computation.13 | async-start | bytes 1327104 | tf_op jit(solution)/shard_map/all_gather | solution.py:132
  223.2 106.2 %all-gather.8.cloned.1.call-start = ((), (), s32[]{:S(2)}) async-start(), calls=%async_computation.14 | async-start | bytes 1327104 | tf_op jit(solution)/shard_map/all_gather | solution.py:134
  223.8 131.1 %reduce-scatter.22.cloned.1.call-start = ((), (), s32[]{:S(2)}) async-start(), calls=%async_computation.15 | async-start | bytes 983040 | tf_op jit(solution)/shard_map/reduce_scatter | solution.py:178
  244.8 149.3 %copy-start.29 = (f32[128]{0:T(128)}, f32[128]{0:T(128)S(1)}, u32[]{:S(2)}) copy-start(f32[128]{0:T(128)S(1)} %broadcast_multiply_fusion.1) | copy-start | bytes 1540
  246.0 148.1 %copy-start.30 = (f32[128]{0:T(128)}, f32[128]{0:T(128)S(1)}, u32[]{:S(2)}) copy-start(f32[128]{0:T(128)S(1)} %fusion.39) | copy-start | bytes 1540
  329.4 25.5 %copy-start.4 = (bf16[128,768]{1,0:T(8,128)(2,1)S(1)}, bf16[128,768]{1,0:T(8,128)(2,1)}, u32[]{:S(2)}) copy-start(bf16[128,768]{1,0:T(8,128)(2,1)} %reduce-scatter.20.cloned.1.call-done) | copy-start | bytes 589828
  332.7 23.7 %copy-start.15 = (bf16[128,768]{1,0:T(8,128)(2,1)S(1)}, bf16[128,768]{1,0:T(8,128)(2,1)}, u32[]{:S(2)}) copy-start(bf16[128,768]{1,0:T(8,128)(2,1)} %param.32) | copy-start | bytes 589828
  332.7 23.7 %copy-start.27 = (f32[768]{0:T(1024)S(1)}, f32[768]{0:T(1024)}, u32[]{:S(2)}) copy-start(f32[768]{0:T(1024)} %param.28) | copy-start | bytes 9220
  332.7 24.0 %copy-start.33 = (f32[768]{0:T(1024)S(1)}, f32[768]{0:T(1024)}, u32[]{:S(2)}) copy-start(f32[768]{0:T(1024)} %param.29) | copy-start | bytes 9220
  332.7 61.4 %reduce-scatter.24.cloned.1.call-start = ((), (), s32[]{:S(2)}) async-start(), calls=%async_computation.16 | async-start | bytes 983040 | tf_op jit(solution)/shard_map/reduce_scatter | solution.py:195
  354.9 11.0 %copy-start.43 = (f32[512,768]{1,0:T(8,128)S(1)}, f32[512,768]{1,0:T(8,128)}, u32[]{:S(2)}) copy-start(f32[512,768]{1,0:T(8,128)} %get-tuple-element.88) | copy-start | bytes 4718596
  356.4 9.5 copy-start.40
  356.4 9.5 copy-start.42
  357.6 36.5 %copy-start.32 = (f32[128]{0:T(128)}, f32[128]{0:T(128)S(1)}, u32[]{:S(2)}) copy-start(f32[128]{0:T(128)S(1)} %negate_multiply_fusion.2) | copy-start | bytes 1540
  365.9 2.7 copy-start.39
  370.3 219.3 %reduce-scatter.26.cloned.1.call-start = ((), (), s32[]{:S(2)}) async-start(), calls=%async_computation.17 | async-start | bytes 7077888 | tf_op jit(solution)/shard_map/reduce_scatter | solution.py:227
  395.9 10.0 copy-start.6
  397.3 9.8 copy-start.1
  397.3 9.8 copy-start.31
  397.3 22.7 %copy-start.35 = (f32[128]{0:T(128)}, f32[128]{0:T(128)S(1)}, u32[]{:S(2)}) copy-start(f32[128]{0:T(128)S(1)} %negate_multiply_fusion.1) | copy-start | bytes 1540
  458.9 8.7 copy-start.7
  470.8 242.7 %reduce-scatter.40.cloned.1.call-start = ((), (), s32[]{:S(2)}) async-start(), calls=%async_computation.24 | async-start | bytes 884736
  473.1 242.0 %reduce-scatter.28.cloned.1.call-start = ((), (), s32[]{:S(2)}) async-start(), calls=%async_computation.18 | async-start | bytes 983040 | tf_op jit(solution)/shard_map/reduce_scatter | solution.py:230
  590.8 3.4 copy-start.11
  590.9 3.4 copy-start.12
  594.2 159.5 %reduce-scatter.32.cloned.1.call-start = ((), (), s32[]{:S(2)}) async-start(), calls=%async_computation.20 | async-start | bytes 2654208 | tf_op jit(solution)/shard_map/reduce_scatter | solution.py:247
  596.5 229.8 %reduce-scatter.30.cloned.1.call-start = ((), (), s32[]{:S(2)}) async-start(), calls=%async_computation.19 | async-start | bytes 2654208 | tf_op jit(solution)/shard_map/reduce_scatter | solution.py:245
  599.8 292.0 %reduce-scatter.38.cloned.1.call-start = ((), (), s32[]{:S(2)}) async-start(), calls=%async_computation.23 | async-start | bytes 884736
  602.9 354.3 %reduce-scatter.36.cloned.1.call-start = ((), (), s32[]{:S(2)}) async-start(), calls=%async_computation.22 | async-start | bytes 884736
  604.1 418.4 %reduce-scatter.34.cloned.1.call-start = ((), (), s32[]{:S(2)}) async-start(), calls=%async_computation.21 | async-start | bytes 884736
  621.1 16.9 %copy-start.34 = (f32[768]{0:T(1024)S(1)}, f32[768]{0:T(1024)}, u32[]{:S(2)}) copy-start(f32[768]{0:T(1024)} %get-tuple-element.89) | copy-start | bytes 9220
  658.3 16.9 %copy-start.28 = (f32[768]{0:T(1024)S(1)}, f32[768]{0:T(1024)}, u32[]{:S(2)}) copy-start(f32[768]{0:T(1024)} %get-tuple-element.64) | copy-start | bytes 9220
  658.3 56.8 %copy-start.36 = (f32[128]{0:T(128)S(1)}, f32[128]{0:T(128)}, u32[]{:S(2)}) copy-start(f32[128]{0:T(128)} %copy-done.35) | copy-start | bytes 1540
  (10 other events, 12.8 us)
Sparse Core Ops, SparseCore 0:
  113.5 67.3 all-gather.3
  222.6 21.1 reduce-scatter.19
  246.2 41.0 all-gather.5
  289.6 39.8 all-gather.7
  332.9 21.9 reduce-scatter.21
  370.4 23.6 reduce-scatter.23
  470.9 118.7 reduce-scatter.25
  593.3 61.5 reduce-scatter.39
  657.5 22.2 reduce-scatter.27
  684.1 69.5 reduce-scatter.31
  758.2 68.0 reduce-scatter.29
  830.4 61.4 reduce-scatter.37
  895.7 61.3 reduce-scatter.35
  961.2 61.2 reduce-scatter.33
where the time goes:
time: 1040 us; the launch traced here: 1030 us
  waiting for transfers between devices  527 us (51%)
  blocking collectives  238 us (23%)
  matrix products  120 us (12%)
  local copies, waits for them, and re-layouts  81.7 us (8%)
  other arithmetic  45.5 us (4%)
  between operations  16.1 us (2%)
    unnamed x18, waiting for transfers between devices  198 us
    reduce_scatter x1, waiting for transfers between devices, shards(): own_grads = lax.psum_scatter(placed, 'dp', scatter_dimension=0, tiled=True)  109 us
    unnamed x101, local copies, waits for them, and re-layouts  78.4 us
    reduce_scatter x1, waiting for transfers between devices, shards(): lax.psum_scatter(grad_w_inner, 'dp', scatter_dimension=0, tiled=True)  72.6 us
    sub x1, matrix products, run(): grad_weight - jnp.sum(attention_weight * grad_weight, axis=-1, keepdims=T...  38.9 us
    psum x1, blocking collectives, shards(): lax.psum((grad_gain_one, grad_shift_one, grad_gain_two, grad_shift_two),...  38.2 us
    unnamed x2, blocking collectives  37.5 us
    reduce_scatter x1, waiting for transfers between devices, shards(): lax.psum_scatter(grad_w_outer, 'dp', scatter_dimension=0, tiled=True)  36.8 us
  transfers between devices with their start and end apart: 14, of which 12 were waited for; matrix products, arithmetic and copies ran while one was open for 12% of the time, Pallas kernels for 0%

commit v1 on v0

--- a/solution.py
+++ b/solution.py
@@ -246,9 +246,8 @@
         lax.psum_scatter(grad_bias, "dp", scatter_dimension=0, tiled=True),
         lax.psum_scatter(grad_w_outer, "dp", scatter_dimension=0, tiled=True),
     )
-    norm_grads = lax.psum(
-        (grad_gain_one, grad_shift_one, grad_gain_two, grad_shift_two), ("dp", "tensor")
-    )
+    partial = lax.psum((grad_gain_one, grad_shift_one, grad_gain_two, grad_shift_two), "tensor")
+    norm_grads = lax.psum(partial, "dp")
     return (
         result.astype(jnp.bfloat16),
         logits,

time: 1040 us -> 1040 us (level)
  blocking collectives: 238 us -> 227 us
  waiting for transfers between devices: 527 us -> 538 us
    psum x1, blocking collectives: 38.2 us -> 10.1 us  [shards(): lax.psum((grad_gain_one, grad_shift_one, grad_gain_two, grad_shift_two),...]
    unnamed x2, blocking collectives: 37.5 us -> 54.8 us
    reduce_scatter x1, waiting for transfers between devices: 36.8 us -> 47.2 us  [shards(): lax.psum_scatter(grad_w_outer, 'dp', scatter_dimension=0, tiled=True)]
where the time goes in v1:
time: 1040 us; the launch traced here: 1030 us
  waiting for transfers between devices  538 us (52%)
  blocking collectives  227 us (22%)
  matrix products  120 us (12%)
  local copies, waits for them, and re-layouts  81.7 us (8%)
  other arithmetic  45.5 us (4%)
  between operations  16.1 us (2%)
    unnamed x18, waiting for transfers between devices  198 us
    reduce_scatter x1, waiting for transfers between devices, shards(): own_grads = lax.psum_scatter(placed, 'dp', scatter_dimension=0, tiled=True)  109 us
    unnamed x101, local copies, waits for them, and re-layouts  78.4 us
    reduce_scatter x1, waiting for transfers between devices, shards(): lax.psum_scatter(grad_w_inner, 'dp', scatter_dimension=0, tiled=True)  72.7 us
    unnamed x2, blocking collectives  54.8 us
    reduce_scatter x1, waiting for transfers between devices, shards(): lax.psum_scatter(grad_w_outer, 'dp', scatter_dimension=0, tiled=True)  47.2 us
    sub x1, matrix products, run(): grad_weight - jnp.sum(attention_weight * grad_weight, axis=-1, keepdims=T...  38.8 us
    all_gather x1, waiting for transfers between devices, shards(): lax.all_gather(w_ffn_out, 'dp', axis=0, tiled=True)  35.6 us
  transfers between devices with their start and end apart: 14, of which 12 were waited for; matrix products, arithmetic and copies ran while one was open for 12% of the time, Pallas kernels for 0%

profile of v1, /device:TPU:0, one launch (start us, length us, event | category | flops | bytes accessed | tf_op | source)
XLA Modules:
  0.0 1029.0 jit_solution(65879327940507813)
XLA Ops:
  7.2 33.0 %all_gather.36 = bf16[768,192]{1,0:T(8,128)(2,1)S(1)} all-gather(bf16[96,192]{1,0:T(8,128)(2,1)} %param.19), channel_id=1, replica_groups=mesh['dp'=8,'tensor'=4] {'dp'}, dimensions={0}, use_global_device_ids=true | all-gather | bytes 331776 | tf_op jit(solution)/shard_map/all_gather | solution.py:128
  40.2 31.4 %all_gather.37 = bf16[768,192]{1,0:T(8,128)(2,1)S(1)} all-gather(bf16[96,192]{1,0:T(8,128)(2,1)} %param.20), channel_id=1, replica_groups=mesh['dp'=8,'tensor'=4] {'dp'}, dimensions={0}, use_global_device_ids=true | all-gather | bytes 331776 | tf_op jit(solution)/shard_map/all_gather | solution.py:129
  71.6 31.2 %all_gather.38 = bf16[768,192]{1,0:T(8,128)(2,1)S(1)} all-gather(bf16[96,192]{1,0:T(8,128)(2,1)} %param.21), channel_id=1, replica_groups=mesh['dp'=8,'tensor'=4] {'dp'}, dimensions={0}, use_global_device_ids=true | all-gather | bytes 331776 | tf_op jit(solution)/shard_map/all_gather | solution.py:130
  102.7 8.8 all_gather.39
  113.6 16.6 %copy.55 = bf16[512,3,4096]{0,2,1:T(8,128)(2,1)} copy(bf16[512,3,4096]{2,0,1:T(8,128)(2,1)} %param.18) | data formatting | bytes 25165824 | tf_op args[1]
  130.5 32.3 %all_gather.41 = bf16[192,768]{0,1:T(8,128)(2,1)S(1)} all-gather(bf16[192,96]{0,1:T(8,128)(2,1)S(1)} %copy.57), channel_id=1, replica_groups=mesh['dp'=8,'tensor'=4] {'dp'}, dimensions={1}, use_global_device_ids=true | all-gather | bytes 331776 | tf_op jit(solution)/shard_map/all_gather | solution.py:131
  162.8 3.5 compare_or_fusion
  166.3 14.6 %all-gather.4.cloned.1.call-done = bf16[4096,384]{0,1:T(8,128)(2,1)} async-done(((bf16[512,384]{0,1:T(8,128)(2,1)}), bf16[4096,384]{0,1:T(8,128)(2,1)}) %all-gather.4.cloned.1.call-update) | async-done | bytes 3145744 | tf_op jit(solution)/shard_map/all_gather | solution.py:143
  180.9 2.3 fusion.52
  183.4 14.6 %select_reduce_fusion = (f32[512,3]{0,1:T(4,128)S(1)}, f32[512,3,4096]{0,2,1:T(8,128)}) fusion(pred[512,4096]{0,1:T(8,128)(4,1)S(1)} %copy-done, bf16[512,3,4096]{0,2,1:T(8,128)(2,1)} %copy.55, bf16[4096,3,64]{0,2,1:T(8,128)(2,1)S(1)} %bitcast.77, bf16[512,3,64]{0,2,1:T(8,128)(2,1)S(1)} %bitcast.85), kind=kOutput, calls=%fused_computation.13 | convolution fusion | flops 836762112 | bytes 41621504 | tf_op jit(solution)/shard_map/qhe,khe->qhk/dot_general | solution.py:28
  198.0 11.0 %fusion.5 = f32[512,3]{0,1:T(4,128)S(1)} fusion(f32[512,3,4096]{0,2,1:T(8,128)} %get-tuple-element.92, f32[512,3]{0,1:T(4,128)S(1)} %get-tuple-element.91, pred[512,4096]{0,1:T(8,128)(4,1)S(1)} %copy-done), kind=kLoop, calls=%fused_computation.12 | loop fusion | flops 18872832 | bytes 27275264 | tf_op jit(solution)/shard_map/reduce_sum | solution.py:35
  209.0 11.5 %fusion.29 = bf16[3,64,512]{2,1,0:T(8,128)(2,1)S(1)} fusion(bf16[4096,3,64]{0,2,1:T(8,128)(2,1)S(1)} %bitcast.83, f32[512,3,4096]{0,2,1:T(8,128)} %get-tuple-element.92, f32[512,3]{0,1:T(4,128)S(1)} %fusion.5, f32[512,3]{0,1:T(4,128)S(1)} %get-tuple-element.91, pred[512,4096]{0,1:T(8,128)(4,1)S(1)} %copy-done), kind=kOutput, calls=%fused_computation.63 | convolution fusion | flops 830570496 | bytes 29044736 | tf_op jit(solution)/shard_map/qhk,khe->qhe/dot_general | solution.py:39
  225.4 17.8 %all-reduce = bf16[768]{0:T(1024)(128)(2,1)S(1)} all-reduce(bf16[768]{0:T(1024)(128)(2,1)S(1)} %dynamic-update-slice), channel_id=1, replica_groups=mesh['dp'=8,'tensor'=4] {'dp'}, use_global_device_ids=true, to_apply=%add | all-reduce | flops 768 | bytes 3072
  247.1 8.7 all_gather.42
  255.8 31.5 %all-gather.6.cloned.1.call-done = bf16[768,768]{1,0:T(8,128)(2,1)} async-done(((bf16[96,768]{1,0:T(8,128)(2,1)}), bf16[768,768]{1,0:T(8,128)(2,1)}) %all-gather.6.cloned.1.call-update) | async-done | bytes 1179664 | tf_op jit(solution)/shard_map/all_gather | solution.py:132
  287.3 6.5 multiply_convert_fusion
  293.8 35.6 %all-gather.8.cloned.1.call-done = bf16[768,768]{1,0:T(8,128)(2,1)} async-done(((bf16[96,768]{1,0:T(8,128)(2,1)}), bf16[768,768]{1,0:T(8,128)(2,1)}) %all-gather.8.cloned.1.call-update) | async-done | bytes 1179664 | tf_op jit(solution)/shard_map/all_gather | solution.py:134
  329.4 3.3 convolution_convert_fusion.2
  332.8 22.1 %reduce-scatter.22.cloned.1.call-done = bf16[128,768]{1,0:T(8,128)(2,1)} async-done(((bf16[512,768]{1,0:T(8,128)(2,1)}), bf16[128,768]{1,0:T(8,128)(2,1)}) %reduce-scatter.22.cloned.1.call-update) | async-done | bytes 196624 | tf_op jit(solution)/shard_map/reduce_scatter | solution.py:178
  357.7 8.2 all_gather.46
  365.9 1.8 convert_reduce_fusion
  368.6 1.7 convolution_convert_fusion
  370.4 16.6 %copy.58 = bf16[512,3,4096]{0,2,1:T(8,128)(2,1)} copy(bf16[512,3,4096]{2,0,1:T(8,128)(2,1)} %param.33) | data formatting | bytes 25165824 | tf_op args[16]
  387.6 6.5 reduce-scatter.24.cloned.1.call-done
  394.1 1.8 multiply_reduce_fusion
  397.4 8.5 all_gather.47
  407.0 13.0 %fusion.7 = f32[3,64,4096]{2,1,0:T(8,128)} fusion(bf16[512,3,64]{0,2,1:T(8,128)(2,1)S(1)} %bitcast.89, f32[512,3,4096]{0,2,1:T(8,128)} %get-tuple-element.92, f32[512,3]{0,1:T(4,128)S(1)} %copy-done.31, pred[512,4096]{0,1:T(8,128)(4,1)S(1)} %copy-done.1), kind=kOutput, calls=%fused_computation.15 | convolution fusion | flops 824180736 | bytes 30611456 | tf_op jit(solution)/shard_map/qhk,qhe->khe/dot_general | solution.py:63
  420.0 38.8 %fusion.4 = bf16[512,3,4096]{0,2,1:T(8,128)(2,1)} fusion(bf16[512,3,4096]{0,2,1:T(8,128)(2,1)} %copy.58, f32[512,3,4096]{0,2,1:T(8,128)} %get-tuple-element.92, f32[512,3]{0,1:T(4,128)} %log_add_fusion, pred[512,4096]{0,1:T(8,128)(4,1)} %compare_or_fusion, bf16[4096,3,64]{0,2,1:T(8,128)(2,1)} %bitcast.84, bf16[512,3,64]{0,2,1:T(8,128)(2,1)} %bitcast.90), kind=kOutput, calls=%fused_computation.6 | convolution fusion | flops 1679824384 | bytes 54204416 | tf_op jit(solution)/shard_map/sub | solution.py:70
  458.9 8.7 convolution_multiply_fusion
  467.6 3.1 pad_maximum_fusion
  470.8 2.3 convolution_bitcast_fusion.1
  473.3 6.8 fusion.28
  480.2 109.5 %reduce-scatter.26.cloned.1.call-done = f32[512,384]{0,1:T(8,128)} async-done(((f32[4096,384]{0,1:T(8,128)}), f32[512,384]{0,1:T(8,128)}) %reduce-scatter.26.cloned.1.call-update) | async-done | bytes 786448 | tf_op jit(solution)/shard_map/reduce_scatter | solution.py:227
  590.8 3.3 convolution_convert_fusion.3
  594.2 2.2 fusion.56
  597.5 2.3 fusion.55
  606.1 14.9 %select_convert_fusion = bf16[512,3,4096]{0,2,1:T(8,128)(2,1)} fusion(f32[512,3,4096]{0,2,1:T(8,128)} %get-tuple-element.92, pred[512,4096]{0,1:T(8,128)(4,1)S(1)} %copy-done.2), kind=kLoop, calls=%fused_computation.9 | loop fusion | flops 6291456 | bytes 39845888 | tf_op jit(solution)/shard_map/convert_element_type | solution.py:31
  621.0 16.9 %copy.62 = bf16[512,3,4096]{2,0,1:T(8,128)(2,1)} copy(bf16[512,3,4096]{0,2,1:T(8,128)(2,1)} %select_convert_fusion) | data formatting | bytes 25165824
  637.9 16.9 %copy.63 = bf16[512,3,4096]{2,0,1:T(8,128)(2,1)} copy(bf16[512,3,4096]{0,2,1:T(8,128)(2,1)} %fusion.4) | data formatting | bytes 25165824
  654.9 10.1 all-reduce.3
  665.0 37.0 %all-reduce.2 = (f32[768]{0:T(1024)S(1)}, f32[768]{0:T(1024)}, f32[768]{0:T(1024)}, f32[768]{0:T(1024)}, f32[768]{0:T(1024)}) all-reduce(f32[768]{0:T(1024)S(1)} %copy-done.34, f32[768]{0:T(1024)S(1)} %get-tuple-element.71, f32[768]{0:T(1024)S(1)} %get-tuple-element.72, ...), channel_id=12, replica_groups=mesh['dp'=8,'tensor'=4] {'dp'}, use_global_device_ids=true, to_apply=%region_24.25.clone | all-reduce | flops 3840 | bytes 30720
  702.6 1.6 copy.78
  704.2 1.8 convert_add_fusion
  706.0 47.2 %reduce-scatter.32.cloned.1.call-done = f32[96,768]{1,0:T(8,128)} async-done(((f32[768,768]{1,0:T(8,128)}), f32[96,768]{1,0:T(8,128)}) %reduce-scatter.32.cloned.1.call-update) | async-done | bytes 294928 | tf_op jit(solution)/shard_map/reduce_scatter | solution.py:247
  753.3 72.7 %reduce-scatter.30.cloned.1.call-done = f32[96,768]{1,0:T(8,128)} async-done(((f32[768,768]{1,0:T(8,128)}), f32[96,768]{1,0:T(8,128)}) %reduce-scatter.30.cloned.1.call-update) | async-done | bytes 294928 | tf_op jit(solution)/shard_map/reduce_scatter | solution.py:245
  825.9 65.6 %reduce-scatter.38.cloned.1.call-done = f32[96,192]{1,0:T(8,128)} async-done(((f32[768,192]{1,0:T(8,128)}), f32[96,192]{1,0:T(8,128)}) %reduce-scatter.38.cloned.1.call-update) | async-done | bytes 73744
  891.5 65.3 %reduce-scatter.36.cloned.1.call-done = f32[96,192]{1,0:T(8,128)} async-done(((f32[768,192]{1,0:T(8,128)}), f32[96,192]{1,0:T(8,128)}) %reduce-scatter.36.cloned.1.call-update) | async-done | bytes 73744
  956.8 65.5 %reduce-scatter.34.cloned.1.call-done = f32[96,192]{1,0:T(8,128)} async-done(((f32[768,192]{1,0:T(8,128)}), f32[96,192]{1,0:T(8,128)}) %reduce-scatter.34.cloned.1.call-update) | async-done | bytes 73744
  (158 shorter events, 26.1 us)
Async XLA Ops:
  7.2 173.7 %all-gather.4.cloned.1.call-start = ((), (), s32[]{:S(2)}) async-start(), calls=%async_computation.11 | async-start | bytes 3538944 | tf_op jit(solution)/shard_map/all_gather | solution.py:143
  40.2 72.4 %copy-start.19 = (bf16[768,192]{1,0:T(8,128)(2,1)}, bf16[768,192]{1,0:T(8,128)(2,1)S(1)}, u32[]{:S(2)}) copy-start(bf16[768,192]{1,0:T(8,128)(2,1)S(1)} %all_gather.36) | copy-start | bytes 884740
  71.6 41.0 %copy-start.20 = (bf16[768,192]{1,0:T(8,128)(2,1)}, bf16[768,192]{1,0:T(8,128)(2,1)S(1)}, u32[]{:S(2)}) copy-start(bf16[768,192]{1,0:T(8,128)(2,1)S(1)} %all_gather.37) | copy-start | bytes 884740
  102.7 9.8 copy-start.21
  113.4 130.4 %reduce-scatter.20.cloned.1.call-start = ((), (), s32[]{:S(2)}) async-start(), calls=%async_computation.12 | async-start | bytes 983040 | tf_op jit(solution)/shard_map/reduce_scatter | solution.py:164
  113.5 69.7 %copy-start.14 = (bf16[512,192]{0,1:T(8,128)(2,1)}, bf16[512,192]{0,1:T(8,128)(2,1)S(1)}, u32[]{:S(2)}) copy-start(bf16[512,192]{0,1:T(8,128)(2,1)S(1)} %slice.33) | copy-start | bytes 589828
  113.6 16.7 %copy-start.25 = (s32[4096]{0:T(1024)S(1)}, s32[4096]{0:T(1024)}, u32[]{:S(2)}) copy-start(s32[4096]{0:T(1024)} %param.30) | copy-start | bytes 49156
  113.6 16.7 %copy-start.37 = (s32[1,13]{1,0:T(1,128)S(1)}, s32[1,13]{1,0:T(1,128)}, u32[]{:S(2)}) copy-start(s32[1,13]{1,0:T(1,128)} %param.31) | copy-start | bytes 160
  162.8 57.8 %copy-start.5 = (bf16[192,768]{0,1:T(8,128)(2,1)}, bf16[192,768]{0,1:T(8,128)(2,1)S(1)}, u32[]{:S(2)}) copy-start(bf16[192,768]{0,1:T(8,128)(2,1)S(1)} %all_gather.41) | copy-start | bytes 884740
  183.2 25.8 %copy-start.13 = (bf16[4096,192]{0,1:T(8,128)(2,1)}, bf16[4096,192]{0,1:T(8,128)(2,1)S(1)}, u32[]{:S(2)}) copy-start(bf16[4096,192]{0,1:T(8,128)(2,1)S(1)} %get-tuple-element.84) | copy-start | bytes 4718596
  220.5 3.4 copy-start.38
  220.5 4.6 copy-start.41
  220.5 23.3 %copy-start.3 = (bf16[128,768]{1,0:T(8,128)(2,1)S(1)}, bf16[128,768]{1,0:T(8,128)(2,1)}, u32[]{:S(2)}) copy-start(bf16[128,768]{1,0:T(8,128)(2,1)} %param.17) | copy-start | bytes 589828
  221.2 24.8 %copy-start.23 = (f32[768]{0:T(1024)S(1)}, f32[768]{0:T(1024)}, u32[]{:S(2)}) copy-start(f32[768]{0:T(1024)} %param.26) | copy-start | bytes 9220
  221.2 24.8 %copy-start.26 = (f32[768]{0:T(1024)S(1)}, f32[768]{0:T(1024)}, u32[]{:S(2)}) copy-start(f32[768]{0:T(1024)} %param.27) | copy-start | bytes 9220
  222.5 64.8 %all-gather.6.cloned.1.call-start = ((), (), s32[]{:S(2)}) async-start(), calls=%async_computation.13 | async-start | bytes 1327104 | tf_op jit(solution)/shard_map/all_gather | solution.py:132
  223.2 106.2 %all-gather.8.cloned.1.call-start = ((), (), s32[]{:S(2)}) async-start(), calls=%async_computation.14 | async-start | bytes 1327104 | tf_op jit(solution)/shard_map/all_gather | solution.py:134
  223.8 131.1 %reduce-scatter.22.cloned.1.call-start = ((), (), s32[]{:S(2)}) async-start(), calls=%async_computation.15 | async-start | bytes 983040 | tf_op jit(solution)/shard_map/reduce_scatter | solution.py:178
  244.8 149.3 %copy-start.29 = (f32[128]{0:T(128)}, f32[128]{0:T(128)S(1)}, u32[]{:S(2)}) copy-start(f32[128]{0:T(128)S(1)} %broadcast_multiply_fusion.1) | copy-start | bytes 1540
  246.0 148.1 %copy-start.30 = (f32[128]{0:T(128)}, f32[128]{0:T(128)S(1)}, u32[]{:S(2)}) copy-start(f32[128]{0:T(128)S(1)} %fusion.39) | copy-start | bytes 1540
  329.4 25.4 %copy-start.4 = (bf16[128,768]{1,0:T(8,128)(2,1)S(1)}, bf16[128,768]{1,0:T(8,128)(2,1)}, u32[]{:S(2)}) copy-start(bf16[128,768]{1,0:T(8,128)(2,1)} %reduce-scatter.20.cloned.1.call-done) | copy-start | bytes 589828
  332.7 23.7 %copy-start.15 = (bf16[128,768]{1,0:T(8,128)(2,1)S(1)}, bf16[128,768]{1,0:T(8,128)(2,1)}, u32[]{:S(2)}) copy-start(bf16[128,768]{1,0:T(8,128)(2,1)} %param.32) | copy-start | bytes 589828
  332.7 23.7 %copy-start.27 = (f32[768]{0:T(1024)S(1)}, f32[768]{0:T(1024)}, u32[]{:S(2)}) copy-start(f32[768]{0:T(1024)} %param.28) | copy-start | bytes 9220
  332.7 24.0 %copy-start.33 = (f32[768]{0:T(1024)S(1)}, f32[768]{0:T(1024)}, u32[]{:S(2)}) copy-start(f32[768]{0:T(1024)} %param.29) | copy-start | bytes 9220
  332.7 61.4 %reduce-scatter.24.cloned.1.call-start = ((), (), s32[]{:S(2)}) async-start(), calls=%async_computation.16 | async-start | bytes 983040 | tf_op jit(solution)/shard_map/reduce_scatter | solution.py:195
  354.9 11.0 %copy-start.43 = (f32[512,768]{1,0:T(8,128)S(1)}, f32[512,768]{1,0:T(8,128)}, u32[]{:S(2)}) copy-start(f32[512,768]{1,0:T(8,128)} %get-tuple-element.93) | copy-start | bytes 4718596
  356.4 9.5 copy-start.40
  356.4 9.5 copy-start.42
  357.6 36.5 %copy-start.32 = (f32[128]{0:T(128)}, f32[128]{0:T(128)S(1)}, u32[]{:S(2)}) copy-start(f32[128]{0:T(128)S(1)} %negate_multiply_fusion.2) | copy-start | bytes 1540
  365.9 2.7 copy-start.39
  370.3 219.3 %reduce-scatter.26.cloned.1.call-start = ((), (), s32[]{:S(2)}) async-start(), calls=%async_computation.17 | async-start | bytes 7077888 | tf_op jit(solution)/shard_map/reduce_scatter | solution.py:227
  395.9 10.0 copy-start.6
  397.3 9.8 copy-start.1
  397.3 9.8 copy-start.31
  397.3 22.7 %copy-start.35 = (f32[128]{0:T(128)}, f32[128]{0:T(128)S(1)}, u32[]{:S(2)}) copy-start(f32[128]{0:T(128)S(1)} %negate_multiply_fusion.1) | copy-start | bytes 1540
  458.9 8.7 copy-start.7
  470.7 231.9 %reduce-scatter.40.cloned.1.call-start = ((), (), s32[]{:S(2)}) async-start(), calls=%async_computation.24 | async-start | bytes 884736
  473.1 231.2 %reduce-scatter.28.cloned.1.call-start = ((), (), s32[]{:S(2)}) async-start(), calls=%async_computation.18 | async-start | bytes 983040 | tf_op jit(solution)/shard_map/reduce_scatter | solution.py:230
  590.8 3.4 copy-start.11
  590.8 3.4 copy-start.12
  594.1 159.1 %reduce-scatter.32.cloned.1.call-start = ((), (), s32[]{:S(2)}) async-start(), calls=%async_computation.20 | async-start | bytes 2654208 | tf_op jit(solution)/shard_map/reduce_scatter | solution.py:247
  596.4 229.5 %reduce-scatter.30.cloned.1.call-start = ((), (), s32[]{:S(2)}) async-start(), calls=%async_computation.19 | async-start | bytes 2654208 | tf_op jit(solution)/shard_map/reduce_scatter | solution.py:245
  599.8 291.7 %reduce-scatter.38.cloned.1.call-start = ((), (), s32[]{:S(2)}) async-start(), calls=%async_computation.23 | async-start | bytes 884736
  602.8 353.9 %reduce-scatter.36.cloned.1.call-start = ((), (), s32[]{:S(2)}) async-start(), calls=%async_computation.22 | async-start | bytes 884736
  604.1 418.1 %reduce-scatter.34.cloned.1.call-start = ((), (), s32[]{:S(2)}) async-start(), calls=%async_computation.21 | async-start | bytes 884736
  637.9 16.9 %copy-start.28 = (f32[768]{0:T(1024)S(1)}, f32[768]{0:T(1024)}, u32[]{:S(2)}) copy-start(f32[768]{0:T(1024)} %get-tuple-element.64) | copy-start | bytes 9220
  637.9 27.1 %copy-start.34 = (f32[768]{0:T(1024)S(1)}, f32[768]{0:T(1024)}, u32[]{:S(2)}) copy-start(f32[768]{0:T(1024)} %get-tuple-element.94) | copy-start | bytes 9220
  637.9 66.3 %copy-start.36 = (f32[128]{0:T(128)S(1)}, f32[128]{0:T(128)}, u32[]{:S(2)}) copy-start(f32[128]{0:T(128)} %copy-done.35) | copy-start | bytes 1540
  (10 other events, 12.8 us)
Sparse Core Ops, SparseCore 0:
  113.5 67.3 all-gather.3
  222.6 21.1 reduce-scatter.19
  246.2 41.0 all-gather.5
  289.6 39.8 all-gather.7
  332.8 21.9 reduce-scatter.21
  370.4 23.6 reduce-scatter.23
  470.8 118.7 reduce-scatter.25
  593.3 61.5 reduce-scatter.39
  657.5 22.2 reduce-scatter.27
  684.0 69.1 reduce-scatter.31
  757.7 68.1 reduce-scatter.29
  830.0 61.4 reduce-scatter.37
  895.4 61.3 reduce-scatter.35
  960.9 61.3 reduce-scatter.33
